TPU v7x, 512 devices: a whole 4x4x16 slice. The times are simulated.
512 devices in a mesh: row: 8 (over z_hi, core), col: 16 (over y, z_lo), depth: 4 (over x).
Axes of the slice: x: 4, y: 4, z: 16 (z_hi: 4, z_lo: 4; z = z_hi * 4 + z_lo), core: 2. Of those that a mesh axis runs over, the one named last changes fastest.
Arguments:
- values: bfloat16 [768, 16, 128, 128], P(('row', 'col')), may hold values from -0.47851562 to 0.47851562
- columns: int32 [768, 16], replicated, may hold values from 0 to 767, as said below
Outputs:
- purified: bfloat16 [768, 16, 128, 128], P(('row', 'col'), 'depth')
Inputs may be any that keep to these rules, and one draw needn't show every extreme that they name: Each block row a names 16 different block columns, a itself among them, all within 8 of a around the cycle of 768 block rows (indices wrap).
All inputs are finite; a program needn't handle non-finite values.
Results may differ from a plain program's by a relative error of at most 0.0047.
Values may be sent and summed in bfloat16 or wider, within the bound.
A program may use at most 128 MiB of HBM per device.

v0:
```python
import jax
import jax.numpy as jnp
from jax import lax
from jax.sharding import PartitionSpec as P

HB = 8


def passed_along(value, axis, by):
    peers = lax.axis_size(axis)
    return lax.ppermute(value, axis, [(i, (i + by) % peers) for i in range(peers)])


def matched_blocks(nearby, band_start, own_cols, target_cols, columns):
    total_blocks = columns.shape[0]
    band_count = nearby.shape[0]
    slot_count = nearby.shape[1]
    partner_cols = jnp.take(columns, own_cols, axis=0)
    same_column = partner_cols[:, :, None, :] == target_cols[:, None, :, None]
    slot_ids = jnp.arange(slot_count, dtype=jnp.int32)
    present = jnp.any(same_column, axis=3)
    chosen = jnp.sum(jnp.where(same_column, slot_ids, 0), axis=3)
    offset = jnp.mod(own_cols - band_start, total_blocks)
    inside = offset < band_count
    usable = inside[:, :, None] & present
    flat_index = jnp.where(
        usable, offset[:, :, None] * slot_count + chosen, band_count * slot_count
    )
    flat_blocks = nearby.reshape(band_count * slot_count, nearby.shape[2], nearby.shape[3])
    return jnp.take(flat_blocks, flat_index, axis=0, mode="fill", fill_value=0)


def local(values, columns):
    own_rows, slot_count, block_size, _ = values.shape
    layers = lax.axis_size("depth")
    quarter = slot_count // layers
    layer_index = lax.axis_index("depth")
    group_index = lax.axis_index(("row", "col"))
    first_row = group_index * own_rows
    own_cols = lax.dynamic_slice_in_dim(columns, first_row, own_rows, 0)
    target_cols = lax.dynamic_slice_in_dim(own_cols, layer_index * quarter, quarter, 1)
    hop_count = (HB + own_rows - 1) // own_rows
    reach_last = HB - (hop_count - 1) * own_rows
    lower_parts = []
    upper_parts = []
    for hop_step in range(1, hop_count + 1):
        edge_rows = own_rows if hop_step < hop_count else reach_last
        from_lower = passed_along(values[own_rows - edge_rows :], ("row", "col"), hop_step)
        from_upper = passed_along(values[:edge_rows], ("row", "col"), -hop_step)
        lower_parts.insert(0, from_lower)
        upper_parts.append(from_upper)
    below_rows = jnp.concatenate(lower_parts, axis=0)
    above_rows = jnp.concatenate(upper_parts, axis=0)
    nearby = jnp.concatenate([below_rows, values, above_rows], axis=0)
    selected = matched_blocks(nearby, first_row - HB, own_cols, target_cols, columns)
    square32 = jnp.einsum("aixy,aijyz->ajxz", values, selected, preferred_element_type=jnp.float32)
    square = square32.astype(jnp.bfloat16)
    whole_square = lax.all_gather(square, "depth", axis=1, tiled=True)
    cube32 = jnp.einsum(
        "aixy,aijyz->ajxz", whole_square, selected, preferred_element_type=jnp.float32
    )
    return (3.0 * square32 - 2.0 * cube32).astype(jnp.bfloat16)


def solution(mesh):
    placed = (P(("row", "col"), None, None, None), P())
    return jax.shard_map(
        local,
        mesh=mesh,
        in_specs=placed,
        out_specs=P(("row", "col"), "depth", None, None),
        check_vma=False,
    )
```

profile of v0, /device:TPU:1, one launch (start us, length us, event | category | flops | bytes accessed | tf_op | source)
XLA Modules:
  0.0 335.9 jit_solution(13076159911926167194)
XLA Ops:
  6.5 4.6 %collective-permute-start.1 = (bf16[6,16,128,128]{3,2,1,0:T(8,128)(2,1)}, bf16[6,16,128,128]{3,2,1,0:T(8,128)(2,1)}, u32[]{:S(2)}, u32[]{:S(2)}) collective-permute-start(bf16[6,16,128,128]{3,2,1,0:T(8,128)(2,1)} %param.2), channel_id=1, source_target_pairs={{0,4},{4,8},{8,12},{12,16},{16,20},{20,24},{24,28},{28,32},{32,36}... | collective-permute-start | bytes 9437192 | tf_op jit(solution)/shard_map/ppermute | solution.py:11
  11.2 7.6 %collective-permute-start.2 = (bf16[6,16,128,128]{3,2,1,0:T(8,128)(2,1)}, bf16[6,16,128,128]{3,2,1,0:T(8,128)(2,1)}, u32[]{:S(2)}, u32[]{:S(2)}) collective-permute-start(bf16[6,16,128,128]{3,2,1,0:T(8,128)(2,1)} %param.2), channel_id=1, source_target_pairs={{0,508},{4,0},{8,4},{12,8},{16,12},{20,16},{24,20},{28,24},{32,28}... | collective-permute-start | bytes 9437192 | tf_op jit(solution)/shard_map/ppermute | solution.py:11
  18.8 3.2 fusion.18
  22.0 1.9 collective-permute-start
  23.9 6.7 %collective-permute-start.3 = (bf16[2,16,128,128]{3,2,1,0:T(8,128)(2,1)}, bf16[2,16,128,128]{3,2,1,0:T(8,128)(2,1)}, u32[]{:S(2)}, u32[]{:S(2)}) collective-permute-start(bf16[2,16,128,128]{3,2,1,0:T(8,128)(2,1)} %get-tuple-element.7), channel_id=1, source_target_pairs={{0,504},{4,508},{8,0},{12,4},{16,8},{20,12},{24,16},{28,20},{32,24... | collective-permute-start | bytes 3145736 | tf_op jit(solution)/shard_map/ppermute | solution.py:11
  30.6 1.0 copy.39
  31.5 0.5 compare_and_fusion.1
  32.1 0.6 reshape.50
  32.7 0.7 pad_clamp_fusion.1
  33.3 1.4 dynamic_slice.7
  34.7 0.8 copy.41
  35.5 1.2 gather_fusion
  36.7 0.9 broadcast_select_fusion.7
  37.6 0.6 compare_reduce_fusion
  38.1 0.6 fusion.14
  38.7 0.1 copy.43
  38.9 0.1 reshape.58
  39.0 0.1 copy.42
  39.1 138.4 %collective-permute-done = bf16[2,16,128,128]{3,2,1,0:T(8,128)(2,1)} collective-permute-done((bf16[2,16,128,128]{3,2,1,0:T(8,128)(2,1)}, bf16[2,16,128,128]{3,2,1,0:T(8,128)(2,1)}, u32[]{:S(2)}, u32[]{:S(2)}) %collective-permute-start) | collective-permute-done | bytes 1048608 | tf_op jit(solution)/shard_map/ppermute | solution.py:11
  177.5 2.4 constant_dynamic-update-slice_fusion.4
  179.8 3.9 %constant_dynamic-update-slice_fusion.3 = bf16[22,16,128,128]{3,2,1,0:T(8,128)(2,1)} fusion(bf16[22,16,128,128]{3,2,1,0:T(8,128)(2,1)} %constant_dynamic-update-slice_fusion.4, bf16[6,16,128,128]{3,2,1,0:T(8,128)(2,1)} %collective-permute-done.1), kind=kLoop, calls=%fused_computation.30 | loop fusion | bytes 6291456
  183.8 2.1 constant_dynamic-update-slice_fusion.2
  185.9 4.0 %constant_dynamic-update-slice_fusion.1 = bf16[22,16,128,128]{3,2,1,0:T(8,128)(2,1)} fusion(bf16[22,16,128,128]{3,2,1,0:T(8,128)(2,1)} %constant_dynamic-update-slice_fusion.2, bf16[6,16,128,128]{3,2,1,0:T(8,128)(2,1)} %collective-permute-done.2), kind=kLoop, calls=%fused_computation.28 | loop fusion | bytes 6291456
  189.8 50.2 %collective-permute-done.3 = bf16[2,16,128,128]{3,2,1,0:T(8,128)(2,1)} collective-permute-done((bf16[2,16,128,128]{3,2,1,0:T(8,128)(2,1)}, bf16[2,16,128,128]{3,2,1,0:T(8,128)(2,1)}, u32[]{:S(2)}, u32[]{:S(2)}) %collective-permute-start.3) | collective-permute-done | bytes 1048608 | tf_op jit(solution)/shard_map/ppermute | solution.py:11
  240.1 2.3 constant_dynamic-update-slice_fusion
  242.4 15.5 %gather_fusion.1 = bf16[384,128,128]{2,1,0:T(8,128)(2,1)} fusion(bf16[352,128,128]{2,1,0:T(8,128)(2,1)} %bitcast.1, s32[1024]{0:T(1024)S(1)} %pad_clamp_fusion), kind=kCustom, calls=%fused_computation.1 | custom fusion | bytes 25167360 | tf_op jit(solution)/shard_map/jit(_take)/gather | solution.py:30
  257.9 7.9 %fusion = f32[6,4,128,128,1]{3,2,1,4,0:T(8,128)S(1)} fusion(bf16[6,16,4,128,128]{4,3,2,1,0:T(8,128)(2,1)} %bitcast.62, pred[6,16,4]{2,1,0:T(8,128)(4,1)S(1)} %copy.42, bf16[6,16,128,128]{3,2,1,0:T(8,128)(2,1)S(1)} %copy-done), kind=kOutput, calls=%fused_computation.3 | convolution fusion | flops 1616904192 | bytes 17301888 | tf_op jit(solution)/shard_map/aixy,aijyz->ajxz/dot_general | solution.py:56
  265.8 1.1 copy-done.1
  266.9 1.0 fusion.13
  268.0 51.1 %all-gather.2.cloned.1.call-done = bf16[6,16,128,128]{2,3,1,0:T(8,128)(2,1)} async-done(((bf16[6,4,128,128]{2,3,1,0:T(8,128)(2,1)}), bf16[6,16,128,128]{2,3,1,0:T(8,128)(2,1)}) %all-gather.2.cloned.1.call-update) | async-done | bytes 3145744 | tf_op jit(solution)/shard_map/all_gather | solution.py:58
  319.1 8.7 %fusion.10 = bf16[6,4,128,128]{2,3,1,0:T(8,128)(2,1)S(1)} fusion(bf16[6,16,128,128]{2,3,1,0:T(8,128)(2,1)} %all-gather.2.cloned.1.call-done, bf16[6,16,4,128,128]{4,3,2,1,0:T(8,128)(2,1)} %bitcast.63, pred[6,16,4]{2,1,0:T(8,128)(4,1)S(1)} %copy.42, f32[6,4,128,128,1]{3,2,1,4,0:T(8,128)} %copy-done.1), kind=kOutput, calls=%fused_computation.14 | convolution fusion | flops 1618477056 | bytes 18088320 | tf_op jit(solution)/shard_map/aixy,aijyz->ajxz/dot_general | solution.py:59
  327.9 1.2 copy.47
  (11 shorter events, 0.1 us)
Async XLA Ops:
  6.5 177.3 %copy-start = (bf16[6,16,128,128]{3,2,1,0:T(8,128)(2,1)S(1)}, bf16[6,16,128,128]{3,2,1,0:T(8,128)(2,1)}, u32[]{:S(2)}) copy-start(bf16[6,16,128,128]{3,2,1,0:T(8,128)(2,1)} %param.2) | copy-start | bytes 9437188
  6.5 312.6 %all-gather.2.cloned.1.call-start = ((), (), s32[]{:S(2)}) async-start(), calls=%async_computation | async-start | bytes 3932160 | tf_op jit(solution)/shard_map/all_gather | solution.py:58
  6.5 173.3 %collective-permute-start.1 = (bf16[6,16,128,128]{3,2,1,0:T(8,128)(2,1)}, bf16[6,16,128,128]{3,2,1,0:T(8,128)(2,1)}, u32[]{:S(2)}, u32[]{:S(2)}) collective-permute-start(bf16[6,16,128,128]{3,2,1,0:T(8,128)(2,1)} %param.2), channel_id=1, source_target_pairs={{0,4},{4,8},{8,12},{12,16},{16,20},{20,24},{24,28},{28,32},{32,36}... | collective-permute-start | bytes 9437192 | tf_op jit(solution)/shard_map/ppermute | solution.py:11
  11.2 174.7 %collective-permute-start.2 = (bf16[6,16,128,128]{3,2,1,0:T(8,128)(2,1)}, bf16[6,16,128,128]{3,2,1,0:T(8,128)(2,1)}, u32[]{:S(2)}, u32[]{:S(2)}) collective-permute-start(bf16[6,16,128,128]{3,2,1,0:T(8,128)(2,1)} %param.2), channel_id=1, source_target_pairs={{0,508},{4,0},{8,4},{12,8},{16,12},{20,16},{24,20},{28,24},{32,28}... | collective-permute-start | bytes 9437192 | tf_op jit(solution)/shard_map/ppermute | solution.py:11
  22.0 155.5 %collective-permute-start = (bf16[2,16,128,128]{3,2,1,0:T(8,128)(2,1)}, bf16[2,16,128,128]{3,2,1,0:T(8,128)(2,1)}, u32[]{:S(2)}, u32[]{:S(2)}) collective-permute-start(bf16[2,16,128,128]{3,2,1,0:T(8,128)(2,1)} %get-tuple-element.8), channel_id=1, source_target_pairs={{0,8},{4,12},{8,16},{12,20},{16,24},{20,28},{24,32},{28,36},{32,40... | collective-permute-start | bytes 3145736 | tf_op jit(solution)/shard_map/ppermute | solution.py:11
  23.9 216.2 %collective-permute-start.3 = (bf16[2,16,128,128]{3,2,1,0:T(8,128)(2,1)}, bf16[2,16,128,128]{3,2,1,0:T(8,128)(2,1)}, u32[]{:S(2)}, u32[]{:S(2)}) collective-permute-start(bf16[2,16,128,128]{3,2,1,0:T(8,128)(2,1)} %get-tuple-element.7), channel_id=1, source_target_pairs={{0,504},{4,508},{8,0},{12,4},{16,8},{20,12},{24,16},{28,20},{32,24... | collective-permute-start | bytes 3145736 | tf_op jit(solution)/shard_map/ppermute | solution.py:11
  265.8 1.1 copy-start.1
Sparse Core Ops, SparseCore 0:
  268.1 50.9 all-gather.1
where the time goes:
time: 336 us
  waiting for transfers between devices  240 us (71%)
  local copies, waits for them, and re-layouts  40.9 us (12%)
  starting transfers between devices  20.8 us (6%)
  matrix products  16.6 us (5%)
  between operations  13.5 us (4%)
  other arithmetic  4.28 us (1%)
    ppermute x4, waiting for transfers between devices, passed_along(): lax.ppermute(value, axis, [(i, (i + by) % peers) for i in range(peers)])  189 us
    all_gather x1, waiting for transfers between devices, local(): whole_square = lax.all_gather(square, 'depth', axis=1, tiled=True)  51.1 us
    ppermute x4, starting transfers between devices, passed_along(): lax.ppermute(value, axis, [(i, (i + by) % peers) for i in range(peers)])  20.8 us
    gather x1, local copies, waits for them, and re-layouts, matched_blocks(): return jnp.take(flat_blocks, flat_index, axis=0, mode='fill', fill_value=0)  15.5 us
    unnamed x9, local copies, waits for them, and re-layouts  14.4 us
    dot_general x1, matrix products, local(): jnp.einsum('aixy,aijyz->ajxz', whole_square, selected, preferred_element_...  8.72 us
    dot_general x1, matrix products, local(): jnp.einsum('aixy,aijyz->ajxz', values, selected, preferred_element_type=j...  7.87 us
  transfers between devices with their start and end apart: 5, of which 3 were waited for; matrix products, arithmetic and copies ran while one was open for 7% of the time, Pallas kernels for 0%

commit v1 on v0

--- a/solution.py
+++ b/solution.py
@@ -55,7 +55,10 @@
     selected = matched_blocks(nearby, first_row - HB, own_cols, target_cols, columns)
     square32 = jnp.einsum("aixy,aijyz->ajxz", values, selected, preferred_element_type=jnp.float32)
     square = square32.astype(jnp.bfloat16)
-    whole_square = lax.all_gather(square, "depth", axis=1, tiled=True)
+    size = lax.axis_size("depth")
+    tiles = jnp.stack([square for _ in range(size)])
+    tiles = lax.all_to_all(tiles, "depth", split_axis=0, concat_axis=0)
+    whole_square = jnp.concatenate(tiles, axis=1)
     cube32 = jnp.einsum(
         "aixy,aijyz->ajxz", whole_square, selected, preferred_element_type=jnp.float32
     )

time: 336 us -> 313 us (0.932)
  waiting for transfers between devices: 240 us -> 190 us
  blocking collectives: 0 us -> 40.4 us
  between operations: 13.5 us -> 0.17 us
    all_gather x1 -> x0, waiting for transfers between devices: 51.1 us -> none  [local(): whole_square = lax.all_gather(square, 'depth', axis=1, tiled=True)]
    all_to_all x0 -> x1, blocking collectives: none -> 40.4 us  [local(): tiles = lax.all_to_all(tiles, 'depth', split_axis=0, concat_axis=0)]
    unnamed x9 -> x11, local copies, waits for them, and re-layouts: 14.4 us -> 14.5 us
  transfers between devices with their start and end apart: 5 -> 4, of which waited for: 3 -> 2; matrix products, arithmetic and copies ran while one was open for 7% -> 7% of each run, Pallas kernels for 0% -> 0%
where the time goes in v1:
time: 313 us; the launch traced here: 312 us
  waiting for transfers between devices  190 us (61%)
  local copies, waits for them, and re-layouts  41.9 us (13%)
  blocking collectives  40.4 us (13%)
  starting transfers between devices  20.8 us (7%)
  matrix products  15.9 us (5%)
    ppermute x4, waiting for transfers between devices, passed_along(): lax.ppermute(value, axis, [(i, (i + by) % peers) for i in range(peers)])  190 us
    all_to_all x1, blocking collectives, local(): tiles = lax.all_to_all(tiles, 'depth', split_axis=0, concat_axis=0)  40.4 us
    ppermute x4, starting transfers between devices, passed_along(): lax.ppermute(value, axis, [(i, (i + by) % peers) for i in range(peers)])  20.8 us
    gather x1, local copies, waits for them, and re-layouts, matched_blocks(): return jnp.take(flat_blocks, flat_index, axis=0, mode='fill', fill_value=0)  15.5 us
    unnamed x11, local copies, waits for them, and re-layouts  14.5 us
    dot_general x1, matrix products, local(): jnp.einsum('aixy,aijyz->ajxz', whole_square, selected, preferred_element_...  7.99 us
    dot_general x1, matrix products, local(): jnp.einsum('aixy,aijyz->ajxz', values, selected, preferred_element_type=j...  7.87 us
  transfers between devices with their start and end apart: 4, of which 2 were waited for; matrix products, arithmetic and copies ran while one was open for 7% of the time, Pallas kernels for 0%

profile of v1, /device:TPU:1, one launch (start us, length us, event | category | flops | bytes accessed | tf_op | source)
XLA Modules:
  0.0 311.7 jit_solution(9051530413614695806)
XLA Ops:
  0.0 4.6 %collective-permute-start.1 = (bf16[6,16,128,128]{3,2,1,0:T(8,128)(2,1)}, bf16[6,16,128,128]{3,2,1,0:T(8,128)(2,1)}, u32[]{:S(2)}, u32[]{:S(2)}) collective-permute-start(bf16[6,16,128,128]{3,2,1,0:T(8,128)(2,1)} %param.2), channel_id=1, source_target_pairs={{0,4},{4,8},{8,12},{12,16},{16,20},{20,24},{24,28},{28,32},{32,36}... | collective-permute-start | bytes 9437192 | tf_op jit(solution)/shard_map/ppermute | solution.py:11
  4.6 7.6 %collective-permute-start.2 = (bf16[6,16,128,128]{3,2,1,0:T(8,128)(2,1)}, bf16[6,16,128,128]{3,2,1,0:T(8,128)(2,1)}, u32[]{:S(2)}, u32[]{:S(2)}) collective-permute-start(bf16[6,16,128,128]{3,2,1,0:T(8,128)(2,1)} %param.2), channel_id=1, source_target_pairs={{0,508},{4,0},{8,4},{12,8},{16,12},{20,16},{24,20},{28,24},{32,28}... | collective-permute-start | bytes 9437192 | tf_op jit(solution)/shard_map/ppermute | solution.py:11
  12.3 3.2 %fusion.13 = (bf16[2,16,128,128]{3,2,1,0:T(8,128)(2,1)}, bf16[2,16,128,128]{3,2,1,0:T(8,128)(2,1)}) fusion(bf16[6,16,128,128]{3,2,1,0:T(8,128)(2,1)} %param.2), kind=kLoop, calls=%fused_computation.40 | loop fusion | bytes 4194304 | tf_op jit(solution)/shard_map/slice | solution.py:49
  15.5 1.9 collective-permute-start
  17.4 6.7 %collective-permute-start.3 = (bf16[2,16,128,128]{3,2,1,0:T(8,128)(2,1)}, bf16[2,16,128,128]{3,2,1,0:T(8,128)(2,1)}, u32[]{:S(2)}, u32[]{:S(2)}) collective-permute-start(bf16[2,16,128,128]{3,2,1,0:T(8,128)(2,1)} %get-tuple-element.7), channel_id=1, source_target_pairs={{0,504},{4,508},{8,0},{12,4},{16,8},{20,12},{24,16},{28,20},{32,24... | collective-permute-start | bytes 3145736 | tf_op jit(solution)/shard_map/ppermute | solution.py:11
  24.0 1.0 copy.53
  25.0 0.6 compare_and_fusion.1
  25.7 1.4 dynamic_slice.7
  27.1 0.8 copy.55
  27.8 1.2 gather_fusion
  29.0 0.9 broadcast_select_fusion.7
  29.9 0.6 compare_reduce_fusion
  30.5 0.6 fusion.9
  31.1 0.1 copy.57
  31.3 0.1 copy.56
  31.5 139.5 %collective-permute-done = bf16[2,16,128,128]{3,2,1,0:T(8,128)(2,1)} collective-permute-done((bf16[2,16,128,128]{3,2,1,0:T(8,128)(2,1)}, bf16[2,16,128,128]{3,2,1,0:T(8,128)(2,1)}, u32[]{:S(2)}, u32[]{:S(2)}) %collective-permute-start) | collective-permute-done | bytes 1048608 | tf_op jit(solution)/shard_map/ppermute | solution.py:11
  170.9 2.4 constant_dynamic-update-slice_fusion.4
  173.3 3.9 %constant_dynamic-update-slice_fusion.3 = bf16[22,16,128,128]{3,2,1,0:T(8,128)(2,1)} fusion(bf16[22,16,128,128]{3,2,1,0:T(8,128)(2,1)} %constant_dynamic-update-slice_fusion.4, bf16[6,16,128,128]{3,2,1,0:T(8,128)(2,1)} %collective-permute-done.1), kind=kLoop, calls=%fused_computation.29 | loop fusion | bytes 6291456
  177.3 2.1 constant_dynamic-update-slice_fusion.2
  179.3 4.0 %constant_dynamic-update-slice_fusion.1 = bf16[22,16,128,128]{3,2,1,0:T(8,128)(2,1)} fusion(bf16[22,16,128,128]{3,2,1,0:T(8,128)(2,1)} %constant_dynamic-update-slice_fusion.2, bf16[6,16,128,128]{3,2,1,0:T(8,128)(2,1)} %collective-permute-done.2), kind=kLoop, calls=%fused_computation.27 | loop fusion | bytes 6291456
  183.3 50.3 %collective-permute-done.3 = bf16[2,16,128,128]{3,2,1,0:T(8,128)(2,1)} collective-permute-done((bf16[2,16,128,128]{3,2,1,0:T(8,128)(2,1)}, bf16[2,16,128,128]{3,2,1,0:T(8,128)(2,1)}, u32[]{:S(2)}, u32[]{:S(2)}) %collective-permute-start.3) | collective-permute-done | bytes 1048608 | tf_op jit(solution)/shard_map/ppermute | solution.py:11
  233.5 2.3 constant_dynamic-update-slice_fusion
  235.9 15.5 %gather_fusion.1 = bf16[384,128,128]{2,1,0:T(8,128)(2,1)} fusion(bf16[352,128,128]{2,1,0:T(8,128)(2,1)} %bitcast.1, s32[1024]{0:T(1024)S(1)} %pad_clamp_fusion), kind=kCustom, calls=%fused_computation.1 | custom fusion | bytes 25167360 | tf_op jit(solution)/shard_map/jit(_take)/gather | solution.py:30
  251.4 7.9 %fusion = f32[6,4,128,128,1]{3,2,1,4,0:T(8,128)S(1)} fusion(bf16[6,16,4,128,128]{4,3,2,1,0:T(8,128)(2,1)} %bitcast.61, pred[6,16,4]{2,1,0:T(8,128)(4,1)S(1)} %copy.56, bf16[6,16,128,128]{3,2,1,0:T(8,128)(2,1)S(1)} %copy-done), kind=kOutput, calls=%fused_computation.3 | convolution fusion | flops 1616904192 | bytes 17301888 | tf_op jit(solution)/shard_map/aixy,aijyz->ajxz/dot_general | solution.py:56
  259.3 1.2 copy-done.1
  260.5 0.1 fusion.8
  260.7 0.4 copy.59
  261.0 0.8 stack.2
  261.9 40.4 %all_to_all.5 = bf16[4,6,4,128,128]{4,3,2,1,0:T(8,128)(2,1)S(1)} all-to-all(bf16[4,6,4,128,128]{4,3,2,1,0:T(8,128)(2,1)S(1)} %stack.2), channel_id=1, replica_groups=mesh['row'=8,'col'=16,'depth'=4] {'depth'}, dimensions={0} | all-to-all | bytes 6291456 | tf_op jit(solution)/shard_map/all_to_all | solution.py:60
  302.3 0.2 copy.60
  302.5 8.0 %fusion.7 = bf16[6,4,128,128]{2,3,1,0:T(8,128)(2,1)S(1)} fusion(bf16[6,16,128,128,1]{3,2,4,1,0:T(8,128)(2,1)S(1)} %bitcast.63, bf16[6,16,4,128,128]{4,3,2,1,0:T(8,128)(2,1)} %bitcast.62, pred[6,16,4]{2,1,0:T(8,128)(4,1)S(1)} %copy.56, f32[6,4,128,128,1]{3,2,1,4,0:T(8,128)S(1)} %copy-done.2), kind=kOutput, calls=%fused_computation.13 | convolution fusion | flops 1618477056 | bytes 18088320 | tf_op jit(solution)/shard_map/aixy,aijyz->ajxz/dot_general | solution.py:62
  310.5 1.2 copy.62
  (14 shorter events, 0.3 us)
Async XLA Ops:
  0.0 177.2 %copy-start = (bf16[6,16,128,128]{3,2,1,0:T(8,128)(2,1)S(1)}, bf16[6,16,128,128]{3,2,1,0:T(8,128)(2,1)}, u32[]{:S(2)}) copy-start(bf16[6,16,128,128]{3,2,1,0:T(8,128)(2,1)} %param.2) | copy-start | bytes 9437188
  0.0 173.3 %collective-permute-start.1 = (bf16[6,16,128,128]{3,2,1,0:T(8,128)(2,1)}, bf16[6,16,128,128]{3,2,1,0:T(8,128)(2,1)}, u32[]{:S(2)}, u32[]{:S(2)}) collective-permute-start(bf16[6,16,128,128]{3,2,1,0:T(8,128)(2,1)} %param.2), channel_id=1, source_target_pairs={{0,4},{4,8},{8,12},{12,16},{16,20},{20,24},{24,28},{28,32},{32,36}... | collective-permute-start | bytes 9437192 | tf_op jit(solution)/shard_map/ppermute | solution.py:11
  4.6 174.7 %collective-permute-start.2 = (bf16[6,16,128,128]{3,2,1,0:T(8,128)(2,1)}, bf16[6,16,128,128]{3,2,1,0:T(8,128)(2,1)}, u32[]{:S(2)}, u32[]{:S(2)}) collective-permute-start(bf16[6,16,128,128]{3,2,1,0:T(8,128)(2,1)} %param.2), channel_id=1, source_target_pairs={{0,508},{4,0},{8,4},{12,8},{16,12},{20,16},{24,20},{28,24},{32,28}... | collective-permute-start | bytes 9437192 | tf_op jit(solution)/shard_map/ppermute | solution.py:11
  15.5 155.5 %collective-permute-start = (bf16[2,16,128,128]{3,2,1,0:T(8,128)(2,1)}, bf16[2,16,128,128]{3,2,1,0:T(8,128)(2,1)}, u32[]{:S(2)}, u32[]{:S(2)}) collective-permute-start(bf16[2,16,128,128]{3,2,1,0:T(8,128)(2,1)} %get-tuple-element.8), channel_id=1, source_target_pairs={{0,8},{4,12},{8,16},{12,20},{16,24},{20,28},{24,32},{28,36},{32,40... | collective-permute-start | bytes 3145736 | tf_op jit(solution)/shard_map/ppermute | solution.py:11
  17.4 216.2 %collective-permute-start.3 = (bf16[2,16,128,128]{3,2,1,0:T(8,128)(2,1)}, bf16[2,16,128,128]{3,2,1,0:T(8,128)(2,1)}, u32[]{:S(2)}, u32[]{:S(2)}) collective-permute-start(bf16[2,16,128,128]{3,2,1,0:T(8,128)(2,1)} %get-tuple-element.7), channel_id=1, source_target_pairs={{0,504},{4,508},{8,0},{12,4},{16,8},{20,12},{24,16},{28,20},{32,24... | collective-permute-start | bytes 3145736 | tf_op jit(solution)/shard_map/ppermute | solution.py:11
  259.3 1.2 copy-start.1
  260.6 41.8 %copy-start.2 = (f32[6,4,128,128,1]{3,2,1,4,0:T(8,128)S(1)}, f32[6,4,128,128,1]{3,2,1,4,0:T(8,128)}, u32[]{:S(2)}) copy-start(f32[6,4,128,128,1]{3,2,1,4,0:T(8,128)} %copy-done.1) | copy-start | bytes 4718596
